TPU v7x, 32 devices: a whole 2x2x4 slice. The times are simulated.
32 devices in a mesh: row: 4 (over y, x), col: 8 (over z, core).
Axes of the slice: x: 2, y: 2, z: 4, core: 2. Of those that a mesh axis runs over, the one named last changes fastest.
Arguments:
- queries: bfloat16 [3072, 1024], P(('row', 'col')), may hold values from -128 to 128
- keys: bfloat16 [3072, 128], P(('row', 'col')), may hold values from -4 to 4
- values: bfloat16 [3072, 128], P(('row', 'col')), may hold values from -6 to 6
- block_start: int32 [32], P(('row', 'col')), may hold values from 0 to 31, as said below
Outputs:
- attended: float32 [3072, 1024], P(('row', 'col'))
- log_total: float32 [3072, 8], P(('row', 'col'))
Inputs may be any that keep to these rules, and one draw needn't show every extreme that they name: `block_start`: a permutation of 0 to 31.
All inputs are finite; a program needn't handle non-finite values.
Results may differ from a plain program's by a relative error of at most 0.0028.
Values may be sent and summed in bfloat16 or wider, within the bound.
No kernel may reach another device: no remote copies, remote signals or barrier semaphores. Data moves between devices by JAX's collectives and lax.ppermute only.
A program may use at most 64 MiB of HBM per device.

v0:
```python
import jax
import jax.numpy as jnp
from jax import lax
from jax.sharding import PartitionSpec as P


def pick_block(piece_len):
    limit = min(piece_len, 1024)
    for size in range(limit, 0, -1):
        if piece_len % size == 0:
            return size
    return piece_len


def local(queries, keys, values, block_start):
    tokens_here = queries.shape[0]
    head_width = keys.shape[1]
    heads_count = queries.shape[1] // head_width
    scale = head_width ** (-0.5)
    query_rows = queries.reshape(tokens_here * heads_count, head_width)
    query_pos = block_start[0] * tokens_here + jnp.arange(tokens_here, dtype=jnp.int32)
    row_pos = jnp.repeat(query_pos, heads_count)
    all_starts = lax.all_gather(block_start, ("row", "col"), axis=0, tiled=True)
    block_ids = jnp.arange(all_starts.shape[0], dtype=jnp.int32)
    paired = jnp.concatenate([keys, values], axis=1)

    def update(state_now, key_block, key_pos):
        accum, peak, total = state_now
        key_part = key_block[:, :head_width]
        value_part = key_block[:, head_width:]
        scores = (
            lax.dot_general(
                query_rows, key_part, (((1,), (1,)), ((), ())), preferred_element_type=jnp.float32
            )
            * scale
        )
        kept = key_pos[None, :] <= row_pos[:, None]
        scores = jnp.where(kept, scores, -1e30)
        new_peak = jnp.maximum(peak, jnp.max(scores, axis=1))
        rescale = jnp.exp(peak - new_peak)
        weights = jnp.where(kept, jnp.exp(scores - new_peak[:, None]), 0.0)
        total = total * rescale + jnp.sum(weights, axis=1)
        accum = accum * rescale[:, None] + jnp.dot(
            weights.astype(jnp.bfloat16), value_part, preferred_element_type=jnp.float32
        )
        return (accum, new_peak, total)

    rows_all = tokens_here * heads_count
    initial = (
        jnp.zeros((rows_all, head_width), jnp.float32),
        jnp.full((rows_all,), -1e30, jnp.float32),
        jnp.zeros((rows_all,), jnp.float32),
    )
    segment = lax.all_gather(paired, "col", axis=0, tiled=True)
    key_piece = lax.all_gather(segment, "row", axis=0, tiled=True)
    piece_len = key_piece.shape[0]
    block_len = pick_block(piece_len)
    count = piece_len // block_len
    key_index = jnp.arange(piece_len, dtype=jnp.int32)
    owner = key_index // tokens_here
    lookup = jnp.sum(
        jnp.where(owner[:, None] == block_ids[None, :], all_starts[None, :], 0), axis=1
    )
    piece_pos = lookup * tokens_here + key_index % tokens_here

    def turn(index, state_in):
        key_block = lax.dynamic_slice_in_dim(key_piece, index * block_len, block_len, 0)
        key_pos = lax.dynamic_slice_in_dim(piece_pos, index * block_len, block_len, 0)
        state_out = update(state_in, key_block, key_pos)
        return state_out

    accum, peak, total = lax.fori_loop(0, count, turn, initial)
    attended = (accum / total[:, None]).reshape(tokens_here, heads_count * head_width)
    log_total = (peak + jnp.log(total)).reshape(tokens_here, heads_count)
    return (attended, log_total)


def solution(mesh):
    placed = (
        P(("row", "col"), None),
        P(("row", "col"), None),
        P(("row", "col"), None),
        P(("row", "col")),
    )
    return jax.shard_map(
        local,
        mesh=mesh,
        in_specs=placed,
        out_specs=(P(("row", "col"), None), P(("row", "col"), None)),
        check_vma=False,
    )
```

profile of v0, /device:TPU:0, one launch (start us, length us, event | category | flops | bytes accessed | tf_op | source)
XLA Modules:
  0.0 90.7 jit_solution(8929716316011239687)
XLA Ops:
  7.2 0.0 all-gather.2.cloned.1.call-start
  7.2 0.8 pad_maximum_fusion
  8.0 17.3 %all_gather.10 = bf16[768,256]{1,0:T(8,128)(2,1)} all-gather(bf16[96,256]{1,0:T(8,128)(2,1)S(1)} %pad_maximum_fusion), channel_id=1, replica_groups=mesh['row'=4,'col'=8] {'col'}, dimensions={0}, use_global_device_ids=true | all-gather | bytes 442368 | tf_op jit(solution)/shard_map/all_gather | solution.py:54
  25.3 0.0 all-gather.2.cloned.1.call-update
  25.9 0.1 dynamic-update-slice
  26.1 40.3 %all-reduce = s32[32]{0:T(128)S(1)} all-reduce(s32[32]{0:T(128)S(1)} %dynamic-update-slice), channel_id=1, replica_groups=mesh['row'=4,'col'=8] {'row','col'}, use_global_device_ids=true, to_apply=%add | all-reduce | flops 32 | bytes 256
  66.3 1.0 %reshape.34 = bf16[768,128]{1,0:T(8,128)(2,1)S(1)} reshape(bf16[96,1024]{1,0:T(8,128)(2,1)} %param.6) | data formatting | bytes 393216 | tf_op jit(solution)/shard_map/reshape | solution.py:20
  67.4 0.1 select_reduce_fusion
  67.5 0.0 all-gather.2.cloned.1.call-done
  67.6 14.6 %while.18 = (s32[]{:T(128)}, f32[768,128]{1,0:T(8,128)S(1)}, f32[768]{0:T(1024)S(1)}, f32[768]{0:T(1024)S(1)}, s32[3072]{0:T(1024)S(1)}, /*index=5*/bf16[3072,25...) while((s32[]{:T(128)}, f32[768,128]{1,0:T(8,128)S(1)}, ...), condition=%wide.region_4.5_spmd.clone, body=%wide.region_1.4_spmd.clone.sunk | while | flops 415534848 | bytes 11033179 | solution.py:72
  67.6 0.1 broadcast_in_dim.88
  67.7 0.1 le.85
  67.8 1.6 %fusion.37 = (f32[768]{0:T(1024)S(1)}, f32[1024,768]{1,0:T(8,128)S(1)}) fusion(s32[768]{0:T(1024)S(1)} %le.85, s32[1024]{0:T(1024)S(1)} %dynamic_slice.17, bf16[768,128]{1,0:T(8,128)(2,1)S(1)} %get-tuple-element.289, bf16[3072,256]{1,0:T(8,128)(2,1)} %get-tuple-element.288, s32[]{:T(128)S(6)} %select_n.85), kind=kOutput, calls=%fused_computation.3.clone.1 | convolution fusion | flops 204471552 | bytes 3614724 | tf_op jit(solution)/shard_map/while/body/eval_jaxpr/dot_general | solution.py:32
  69.4 0.9 fusion.38
  70.3 2.1 %fusion.40 = f32[768,128]{1,0:T(8,128)S(1)} fusion(f32[1024,768]{1,0:T(8,128)S(1)} %get-tuple-element.253, f32[768]{0:T(1024)S(1)} %select_maximum_fusion.2, s32[768]{0:T(1024)S(1)} %le.85, s32[1024]{0:T(1024)S(1)} %dynamic_slice.17, f32[768,128]{1,0:T(8,128)S(1)} %get-tuple-element.271, bf16[3072,256]{1,0:T(8,128)(2,1)} %get-tuple-element.288, ...), kind=kOutput, calls=%fused_computation.7.clone.1 | convolution fusion | flops 206340096 | bytes 4207625 | tf_op jit(solution)/shard_map/while/body/eval_jaxpr/dot_general | solution.py:43
  72.5 0.1 broadcast_in_dim.88
  72.5 0.1 le.85
  72.6 1.6 %fusion.37 = (f32[768]{0:T(1024)S(1)}, f32[1024,768]{1,0:T(8,128)S(1)}) fusion(s32[768]{0:T(1024)S(1)} %le.85, s32[1024]{0:T(1024)S(1)} %dynamic_slice.17, bf16[768,128]{1,0:T(8,128)(2,1)S(1)} %get-tuple-element.289, bf16[3072,256]{1,0:T(8,128)(2,1)} %get-tuple-element.288, s32[]{:T(128)S(6)} %select_n.85), kind=kOutput, calls=%fused_computation.3.clone.1 | convolution fusion | flops 204471552 | bytes 3614724 | tf_op jit(solution)/shard_map/while/body/eval_jaxpr/dot_general | solution.py:32
  74.2 0.9 fusion.38
  75.1 2.1 %fusion.40 = f32[768,128]{1,0:T(8,128)S(1)} fusion(f32[1024,768]{1,0:T(8,128)S(1)} %get-tuple-element.253, f32[768]{0:T(1024)S(1)} %select_maximum_fusion.2, s32[768]{0:T(1024)S(1)} %le.85, s32[1024]{0:T(1024)S(1)} %dynamic_slice.17, f32[768,128]{1,0:T(8,128)S(1)} %get-tuple-element.271, bf16[3072,256]{1,0:T(8,128)(2,1)} %get-tuple-element.288, ...), kind=kOutput, calls=%fused_computation.7.clone.1 | convolution fusion | flops 206340096 | bytes 4207625 | tf_op jit(solution)/shard_map/while/body/eval_jaxpr/dot_general | solution.py:43
  77.3 0.1 broadcast_in_dim.88
  77.4 0.1 le.85
  77.5 1.6 %fusion.37 = (f32[768]{0:T(1024)S(1)}, f32[1024,768]{1,0:T(8,128)S(1)}) fusion(s32[768]{0:T(1024)S(1)} %le.85, s32[1024]{0:T(1024)S(1)} %dynamic_slice.17, bf16[768,128]{1,0:T(8,128)(2,1)S(1)} %get-tuple-element.289, bf16[3072,256]{1,0:T(8,128)(2,1)} %get-tuple-element.288, s32[]{:T(128)S(6)} %select_n.85), kind=kOutput, calls=%fused_computation.3.clone.1 | convolution fusion | flops 204471552 | bytes 3614724 | tf_op jit(solution)/shard_map/while/body/eval_jaxpr/dot_general | solution.py:32
  79.1 0.9 fusion.38
  80.0 2.1 %fusion.40 = f32[768,128]{1,0:T(8,128)S(1)} fusion(f32[1024,768]{1,0:T(8,128)S(1)} %get-tuple-element.253, f32[768]{0:T(1024)S(1)} %select_maximum_fusion.2, s32[768]{0:T(1024)S(1)} %le.85, s32[1024]{0:T(1024)S(1)} %dynamic_slice.17, f32[768,128]{1,0:T(8,128)S(1)} %get-tuple-element.271, bf16[3072,256]{1,0:T(8,128)(2,1)} %get-tuple-element.288, ...), kind=kOutput, calls=%fused_computation.7.clone.1 | convolution fusion | flops 206340096 | bytes 4207625 | tf_op jit(solution)/shard_map/while/body/eval_jaxpr/dot_general | solution.py:43
  82.1 0.2 broadcast_divide_fusion
  82.3 0.8 reshape.35
  83.2 0.1 reshape.36
  83.2 0.7 copy.7
  (20 shorter events, 0.1 us)
Async XLA Ops:
  7.2 60.4 %all-gather.2.cloned.1.call-start = ((), (), s32[]{:S(2)}) async-start(), calls=%async_computation | async-start | bytes 1966080 | tf_op jit(solution)/shard_map/all_gather | solution.py:55
Sparse Core Ops, SparseCore 0:
  25.4 32.0 all-gather.1
where the time goes:
time: 91.2 us; the launch traced here: 90.7 us
  blocking collectives  57.6 us (63%)
  between operations  14.8 us (16%)
  matrix products  11.1 us (12%)
  other arithmetic  3.83 us (4%)
  local copies, waits for them, and re-layouts  3.21 us (4%)
    unnamed x1, blocking collectives  40.3 us
    all_gather x1, blocking collectives, local(): segment = lax.all_gather(paired, 'col', axis=0, tiled=True)  17.3 us
    dot_general x3, matrix products, update(): jnp.dot(weights.astype(jnp.bfloat16), value_part, preferred_element_type=...  6.39 us
    dot_general x3, matrix products, update(): lax.dot_general(query_rows, key_part, (((1,), (1,)), ((), ())), preferred...  4.7 us
    reduce_sum x3, other arithmetic, update(): total = total * rescale + jnp.sum(weights, axis=1)  2.67 us
  transfers between devices with their start and end apart: 1, of which 0 were waited for; matrix products, arithmetic and copies ran while one was open for 1% of the time, Pallas kernels for 0%

commit v1 on v0

--- a/solution.py
+++ b/solution.py
@@ -51,7 +51,12 @@
         jnp.full((rows_all,), -1e30, jnp.float32),
         jnp.zeros((rows_all,), jnp.float32),
     )
-    segment = lax.all_gather(paired, "col", axis=0, tiled=True)
+    ring = [paired]
+    for hop in range(7):
+        ring.append(lax.ppermute(ring[-1], "col", [(dev, (dev + 1) % 8) for dev in range(8)]))
+    segment = jnp.roll(
+        jnp.concatenate(ring[::-1], axis=0), (lax.axis_index("col") + 1) * ring[0].shape[0], axis=0
+    )
     key_piece = lax.all_gather(segment, "row", axis=0, tiled=True)
     piece_len = key_piece.shape[0]
     block_len = pick_block(piece_len)

time: 91.2 us -> 115 us (1.26)
  waiting for transfers between devices: 0.04 us -> 37.7 us
  blocking collectives: 57.6 us -> 38.4 us
  local copies, waits for them, and re-layouts: 3.21 us -> 7.12 us
    ppermute x0 -> x7, waiting for transfers between devices: none -> 37.7 us  [local(): lax.ppermute(ring[-1], 'col', [(dev, (dev + 1) % 8) for dev in range(8)])]
    all_gather x1 -> x0, blocking collectives: 17.3 us -> none  [local(): segment = lax.all_gather(paired, 'col', axis=0, tiled=True)]
    unnamed x3 -> x20, local copies, waits for them, and re-layouts: 0.78 us -> 3.1 us
    unnamed x1, blocking collectives: 40.3 us -> 38.4 us
  transfers between devices with their start and end apart: 1 -> 8, of which waited for: 0 -> 7; matrix products, arithmetic and copies ran while one was open for 1% -> 1% of each run, Pallas kernels for 0% -> 0%
where the time goes in v1:
time: 115 us; the launch traced here: 114 us
  blocking collectives  38.4 us (33%)
  waiting for transfers between devices  37.7 us (33%)
  between operations  14.9 us (13%)
  matrix products  11.1 us (10%)
  local copies, waits for them, and re-layouts  7.12 us (6%)
  other arithmetic  3.83 us (3%)
    unnamed x1, blocking collectives  38.4 us
    ppermute x7, waiting for transfers between devices, local(): lax.ppermute(ring[-1], 'col', [(dev, (dev + 1) % 8) for dev in range(8)])  37.7 us
    dot_general x3, matrix products, update(): jnp.dot(weights.astype(jnp.bfloat16), value_part, preferred_element_type=...  6.38 us
    dot_general x3, matrix products, update(): lax.dot_general(query_rows, key_part, (((1,), (1,)), ((), ())), preferred...  4.7 us
    unnamed x20, local copies, waits for them, and re-layouts  3.1 us
    reduce_sum x3, other arithmetic, update(): total = total * rescale + jnp.sum(weights, axis=1)  2.67 us
  transfers between devices with their start and end apart: 8, of which 7 were waited for; matrix products, arithmetic and copies ran while one was open for 1% of the time, Pallas kernels for 0%

profile of v1, /device:TPU:0, one launch (start us, length us, event | category | flops | bytes accessed | tf_op | source)
XLA Modules:
  0.0 113.8 jit_solution(14758420867028339679)
XLA Ops:
  7.2 0.0 all-gather.2.cloned.1.call-start
  7.2 0.8 pad_maximum_fusion
  8.0 0.5 collective-permute-start
  8.5 5.8 %collective-permute-done = bf16[96,256]{1,0:T(8,128)(2,1)S(1)} collective-permute-done((bf16[96,256]{1,0:T(8,128)(2,1)S(1)}, bf16[96,256]{1,0:T(8,128)(2,1)S(1)}, u32[]{:S(2)}, u32[]{:S(2)}) %collective-permute-start) | collective-permute-done | bytes 49184 | tf_op jit(solution)/shard_map/ppermute | solution.py:56
  14.3 0.0 collective-permute-start.1
  14.3 5.3 %collective-permute-done.1 = bf16[96,256]{1,0:T(8,128)(2,1)S(1)} collective-permute-done((bf16[96,256]{1,0:T(8,128)(2,1)S(1)}, bf16[96,256]{1,0:T(8,128)(2,1)S(1)}, u32[]{:S(2)}, u32[]{:S(2)}) %collective-permute-start.1) | collective-permute-done | bytes 49184 | tf_op jit(solution)/shard_map/ppermute | solution.py:56
  19.6 0.0 collective-permute-start.2
  19.6 5.3 %collective-permute-done.2 = bf16[96,256]{1,0:T(8,128)(2,1)S(1)} collective-permute-done((bf16[96,256]{1,0:T(8,128)(2,1)S(1)}, bf16[96,256]{1,0:T(8,128)(2,1)S(1)}, u32[]{:S(2)}, u32[]{:S(2)}) %collective-permute-start.2) | collective-permute-done | bytes 49184 | tf_op jit(solution)/shard_map/ppermute | solution.py:56
  24.9 0.0 collective-permute-start.3
  24.9 5.3 %collective-permute-done.3 = bf16[96,256]{1,0:T(8,128)(2,1)S(1)} collective-permute-done((bf16[96,256]{1,0:T(8,128)(2,1)S(1)}, bf16[96,256]{1,0:T(8,128)(2,1)S(1)}, u32[]{:S(2)}, u32[]{:S(2)}) %collective-permute-start.3) | collective-permute-done | bytes 49184 | tf_op jit(solution)/shard_map/ppermute | solution.py:56
  30.2 0.0 collective-permute-start.4
  30.2 5.3 %collective-permute-done.4 = bf16[96,256]{1,0:T(8,128)(2,1)S(1)} collective-permute-done((bf16[96,256]{1,0:T(8,128)(2,1)S(1)}, bf16[96,256]{1,0:T(8,128)(2,1)S(1)}, u32[]{:S(2)}, u32[]{:S(2)}) %collective-permute-start.4) | collective-permute-done | bytes 49184 | tf_op jit(solution)/shard_map/ppermute | solution.py:56
  35.6 0.0 collective-permute-start.5
  35.6 5.3 %collective-permute-done.5 = bf16[96,256]{1,0:T(8,128)(2,1)S(1)} collective-permute-done((bf16[96,256]{1,0:T(8,128)(2,1)S(1)}, bf16[96,256]{1,0:T(8,128)(2,1)S(1)}, u32[]{:S(2)}, u32[]{:S(2)}) %collective-permute-start.5) | collective-permute-done | bytes 49184 | tf_op jit(solution)/shard_map/ppermute | solution.py:56
  40.9 0.0 collective-permute-start.6
  40.9 5.3 %collective-permute-done.6 = bf16[96,256]{1,0:T(8,128)(2,1)S(1)} collective-permute-done((bf16[96,256]{1,0:T(8,128)(2,1)S(1)}, bf16[96,256]{1,0:T(8,128)(2,1)S(1)}, u32[]{:S(2)}, u32[]{:S(2)}) %collective-permute-start.6) | collective-permute-done | bytes 49184 | tf_op jit(solution)/shard_map/ppermute | solution.py:56
  46.3 0.8 constant_dynamic-update-slice_fusion.8
  47.0 0.7 constant_dynamic-update-slice_fusion.17
  47.9 0.8 constant_dynamic-update-slice_fusion
  48.6 0.7 constant_dynamic-update-slice_fusion.16
  49.4 0.8 constant_dynamic-slice_fusion
  50.2 0.0 all-gather.2.cloned.1.call-update
  50.9 0.1 dynamic-update-slice
  51.0 38.4 %all-reduce = s32[32]{0:T(128)S(1)} all-reduce(s32[32]{0:T(128)S(1)} %dynamic-update-slice), channel_id=1, replica_groups=mesh['row'=4,'col'=8] {'row','col'}, use_global_device_ids=true, to_apply=%add | all-reduce | flops 32 | bytes 256
  89.4 1.0 reshape.34
  90.5 0.1 select_reduce_fusion
  90.6 0.0 all-gather.2.cloned.1.call-done
  90.7 14.6 %while.18 = (s32[]{:T(128)}, f32[768,128]{1,0:T(8,128)S(1)}, f32[768]{0:T(1024)S(1)}, f32[768]{0:T(1024)S(1)}, s32[3072]{0:T(1024)S(1)}, /*index=5*/bf16[3072,25...) while((s32[]{:T(128)}, f32[768,128]{1,0:T(8,128)S(1)}, ...), condition=%wide.region_4.5_spmd.clone, body=%wide.region_1.4_spmd.clone.sunk | while | flops 415534848 | bytes 11033179 | solution.py:77
  90.7 0.1 broadcast_in_dim.88
  90.8 0.1 le.85
  90.9 1.6 %fusion.37 = (f32[768]{0:T(1024)S(1)}, f32[1024,768]{1,0:T(8,128)S(1)}) fusion(s32[768]{0:T(1024)S(1)} %le.85, s32[1024]{0:T(1024)S(1)} %dynamic_slice.23, bf16[768,128]{1,0:T(8,128)(2,1)S(1)} %get-tuple-element.289, bf16[3072,256]{1,0:T(8,128)(2,1)} %get-tuple-element.288, s32[]{:T(128)S(6)} %select_n.99), kind=kOutput, calls=%fused_computation.3.clone.1 | convolution fusion | flops 204471552 | bytes 3614724 | tf_op jit(solution)/shard_map/while/body/eval_jaxpr/dot_general | solution.py:32
  92.4 0.9 fusion.38
  93.4 2.1 %fusion.40 = f32[768,128]{1,0:T(8,128)S(1)} fusion(f32[1024,768]{1,0:T(8,128)S(1)} %get-tuple-element.253, f32[768]{0:T(1024)S(1)} %select_maximum_fusion.2, s32[768]{0:T(1024)S(1)} %le.85, s32[1024]{0:T(1024)S(1)} %dynamic_slice.23, f32[768,128]{1,0:T(8,128)S(1)} %get-tuple-element.271, bf16[3072,256]{1,0:T(8,128)(2,1)} %get-tuple-element.288, ...), kind=kOutput, calls=%fused_computation.7.clone.1 | convolution fusion | flops 206340096 | bytes 4207625 | tf_op jit(solution)/shard_map/while/body/eval_jaxpr/dot_general | solution.py:43
  95.5 0.1 broadcast_in_dim.88
  95.6 0.1 le.85
  95.7 1.6 %fusion.37 = (f32[768]{0:T(1024)S(1)}, f32[1024,768]{1,0:T(8,128)S(1)}) fusion(s32[768]{0:T(1024)S(1)} %le.85, s32[1024]{0:T(1024)S(1)} %dynamic_slice.23, bf16[768,128]{1,0:T(8,128)(2,1)S(1)} %get-tuple-element.289, bf16[3072,256]{1,0:T(8,128)(2,1)} %get-tuple-element.288, s32[]{:T(128)S(6)} %select_n.99), kind=kOutput, calls=%fused_computation.3.clone.1 | convolution fusion | flops 204471552 | bytes 3614724 | tf_op jit(solution)/shard_map/while/body/eval_jaxpr/dot_general | solution.py:32
  97.3 0.9 fusion.38
  98.2 2.1 %fusion.40 = f32[768,128]{1,0:T(8,128)S(1)} fusion(f32[1024,768]{1,0:T(8,128)S(1)} %get-tuple-element.253, f32[768]{0:T(1024)S(1)} %select_maximum_fusion.2, s32[768]{0:T(1024)S(1)} %le.85, s32[1024]{0:T(1024)S(1)} %dynamic_slice.23, f32[768,128]{1,0:T(8,128)S(1)} %get-tuple-element.271, bf16[3072,256]{1,0:T(8,128)(2,1)} %get-tuple-element.288, ...), kind=kOutput, calls=%fused_computation.7.clone.1 | convolution fusion | flops 206340096 | bytes 4207625 | tf_op jit(solution)/shard_map/while/body/eval_jaxpr/dot_general | solution.py:43
  100.4 0.1 broadcast_in_dim.88
  100.5 0.1 le.85
  100.6 1.6 %fusion.37 = (f32[768]{0:T(1024)S(1)}, f32[1024,768]{1,0:T(8,128)S(1)}) fusion(s32[768]{0:T(1024)S(1)} %le.85, s32[1024]{0:T(1024)S(1)} %dynamic_slice.23, bf16[768,128]{1,0:T(8,128)(2,1)S(1)} %get-tuple-element.289, bf16[3072,256]{1,0:T(8,128)(2,1)} %get-tuple-element.288, s32[]{:T(128)S(6)} %select_n.99), kind=kOutput, calls=%fused_computation.3.clone.1 | convolution fusion | flops 204471552 | bytes 3614724 | tf_op jit(solution)/shard_map/while/body/eval_jaxpr/dot_general | solution.py:32
  102.2 0.9 fusion.38
  103.1 2.1 %fusion.40 = f32[768,128]{1,0:T(8,128)S(1)} fusion(f32[1024,768]{1,0:T(8,128)S(1)} %get-tuple-element.253, f32[768]{0:T(1024)S(1)} %select_maximum_fusion.2, s32[768]{0:T(1024)S(1)} %le.85, s32[1024]{0:T(1024)S(1)} %dynamic_slice.23, f32[768,128]{1,0:T(8,128)S(1)} %get-tuple-element.271, bf16[3072,256]{1,0:T(8,128)(2,1)} %get-tuple-element.288, ...), kind=kOutput, calls=%fused_computation.7.clone.1 | convolution fusion | flops 206340096 | bytes 4207625 | tf_op jit(solution)/shard_map/while/body/eval_jaxpr/dot_general | solution.py:43
  105.2 0.2 broadcast_divide_fusion
  105.4 0.8 reshape.35
  106.2 0.1 reshape.36
  106.3 0.7 copy.7
  (34 shorter events, 0.2 us)
Async XLA Ops:
  7.2 83.5 %all-gather.2.cloned.1.call-start = ((), (), s32[]{:S(2)}) async-start(), calls=%async_computation | async-start | bytes 1966080 | tf_op jit(solution)/shard_map/all_gather | solution.py:60
  8.0 6.3 %collective-permute-start = (bf16[96,256]{1,0:T(8,128)(2,1)S(1)}, bf16[96,256]{1,0:T(8,128)(2,1)S(1)}, u32[]{:S(2)}, u32[]{:S(2)}) collective-permute-start(bf16[96,256]{1,0:T(8,128)(2,1)S(1)} %pad_maximum_fusion), channel_id=1, source_target_pairs={{0,1},{1,2},{2,3},{3,4},{4,5},{5,6},{6,7},{7,0},{8,9},{9,10},{10,1... | collective-permute-start | bytes 147464 | tf_op jit(solution)/shard_map/ppermute | solution.py:56
  14.3 5.3 %collective-permute-start.1 = (bf16[96,256]{1,0:T(8,128)(2,1)S(1)}, bf16[96,256]{1,0:T(8,128)(2,1)S(1)}, u32[]{:S(2)}, u32[]{:S(2)}) collective-permute-start(bf16[96,256]{1,0:T(8,128)(2,1)S(1)} %collective-permute-done), channel_id=1, source_target_pairs={{0,1},{1,2},{2,3},{3,4},{4,5},{5,6},{6,7},{7,0},{8,9},{9,10},{10,1... | collective-permute-start | bytes 147464 | tf_op jit(solution)/shard_map/ppermute | solution.py:56
  19.6 5.3 %collective-permute-start.2 = (bf16[96,256]{1,0:T(8,128)(2,1)S(1)}, bf16[96,256]{1,0:T(8,128)(2,1)S(1)}, u32[]{:S(2)}, u32[]{:S(2)}) collective-permute-start(bf16[96,256]{1,0:T(8,128)(2,1)S(1)} %collective-permute-done.1), channel_id=1, source_target_pairs={{0,1},{1,2},{2,3},{3,4},{4,5},{5,6},{6,7},{7,0},{8,9},{9,10},{10,1... | collective-permute-start | bytes 147464 | tf_op jit(solution)/shard_map/ppermute | solution.py:56
  24.9 5.3 %collective-permute-start.3 = (bf16[96,256]{1,0:T(8,128)(2,1)S(1)}, bf16[96,256]{1,0:T(8,128)(2,1)S(1)}, u32[]{:S(2)}, u32[]{:S(2)}) collective-permute-start(bf16[96,256]{1,0:T(8,128)(2,1)S(1)} %collective-permute-done.2), channel_id=1, source_target_pairs={{0,1},{1,2},{2,3},{3,4},{4,5},{5,6},{6,7},{7,0},{8,9},{9,10},{10,1... | collective-permute-start | bytes 147464 | tf_op jit(solution)/shard_map/ppermute | solution.py:56
  30.2 5.3 %collective-permute-start.4 = (bf16[96,256]{1,0:T(8,128)(2,1)S(1)}, bf16[96,256]{1,0:T(8,128)(2,1)S(1)}, u32[]{:S(2)}, u32[]{:S(2)}) collective-permute-start(bf16[96,256]{1,0:T(8,128)(2,1)S(1)} %collective-permute-done.3), channel_id=1, source_target_pairs={{0,1},{1,2},{2,3},{3,4},{4,5},{5,6},{6,7},{7,0},{8,9},{9,10},{10,1... | collective-permute-start | bytes 147464 | tf_op jit(solution)/shard_map/ppermute | solution.py:56
  35.6 5.3 %collective-permute-start.5 = (bf16[96,256]{1,0:T(8,128)(2,1)S(1)}, bf16[96,256]{1,0:T(8,128)(2,1)S(1)}, u32[]{:S(2)}, u32[]{:S(2)}) collective-permute-start(bf16[96,256]{1,0:T(8,128)(2,1)S(1)} %collective-permute-done.4), channel_id=1, source_target_pairs={{0,1},{1,2},{2,3},{3,4},{4,5},{5,6},{6,7},{7,0},{8,9},{9,10},{10,1... | collective-permute-start | bytes 147464 | tf_op jit(solution)/shard_map/ppermute | solution.py:56
  40.9 5.3 %collective-permute-start.6 = (bf16[96,256]{1,0:T(8,128)(2,1)S(1)}, bf16[96,256]{1,0:T(8,128)(2,1)S(1)}, u32[]{:S(2)}, u32[]{:S(2)}) collective-permute-start(bf16[96,256]{1,0:T(8,128)(2,1)S(1)} %collective-permute-done.5), channel_id=1, source_target_pairs={{0,1},{1,2},{2,3},{3,4},{4,5},{5,6},{6,7},{7,0},{8,9},{9,10},{10,1... | collective-permute-start | bytes 147464 | tf_op jit(solution)/shard_map/ppermute | solution.py:56
Sparse Core Ops, SparseCore 0:
  50.3 29.7 all-gather.1
